TPU v7x, 32 devices: a whole 2x2x4 slice. The times are simulated.
32 devices in a mesh: parts: 2 (over y), seq: 4 (over z), chan: 4 (over x, core).
Axes of the slice: x: 2, y: 2, z: 4, core: 2. Of those that a mesh axis runs over, the one named last changes fastest.
Arguments:
- records: bfloat16 [8, 1536, 512], P('parts', 'seq', 'chan'), parts along dimension 0, may hold values from -6 to 6
- norm_gain: float32 [512], replicated, may hold values from 0.1 to 1.9
- in_projection: bfloat16 [512, 3, 512], P(None, None, 'chan'), may hold values from -0.25 to 0.25
- short_kernel: float32 [3, 3, 512], P(None, None, 'chan'), may hold values from -3.5 to 3.5
- long_filter: bfloat16 [16, 1536], P('chan', 'seq'), may hold values from -1.6 to 1.6
- skip_gain: float32 [512], P('chan'), may hold values from 0.5 to 1.5
- out_projection: bfloat16 [512, 512], P('chan'), may hold values from -0.25 to 0.25
Outputs:
- mixed: bfloat16 [8, 1536, 512], P('parts', 'seq', 'chan'), parts along dimension 0
There are 2 independent parts, one for each index of `parts`. A program takes and returns all parts, laid end to end along the dimension named above; an argument that names none is the same for every part. Nothing has to cross between parts.
All inputs are finite; a program needn't handle non-finite values.
Results may differ from a plain program's by a relative error of at most 0.015.
Values may be sent and summed in bfloat16 or wider, within the bound.
A program may use at most 128 MiB of HBM per device.

v0:
```python
import jax
import jax.numpy as jnp
from jax import lax
from jax.sharding import PartitionSpec as P


def from_behind(block, axis, distance):
    devices = range(lax.axis_size(axis))
    route = [(i - distance, i) for i in devices if i - distance in devices]
    return lax.ppermute(block, axis, route)


def block_terms(taps_padded, offset, block_source, block_len):
    filter_count = taps_padded.shape[0]
    window = lax.dynamic_slice_in_dim(taps_padded, offset + 1, 2 * block_len - 1, 1)
    flipped = window[:, ::-1]
    padded = jnp.pad(flipped, ((0, 0), (0, 1)))
    tiled_taps = jnp.tile(padded, (1, block_len))
    toeplitz = tiled_taps[:, block_len - 1 : block_len - 1 + block_len * (2 * block_len - 1)]
    toeplitz = toeplitz.reshape(filter_count, block_len, 2 * block_len - 1)[:, :, :block_len]
    record_count = block_source.shape[0]
    grouped = block_source.reshape(record_count, block_len, filter_count, -1)
    return jnp.einsum("fab,rbfg->rafg", toeplitz, grouped, preferred_element_type=jnp.float32)


def body(records, norm_gain, in_projection, short_kernel, long_filter, skip_gain, out_projection):
    gathered = lax.all_gather(records, "chan", axis=2, tiled=True)
    widened = gathered.astype(jnp.float32)
    inv_rms = lax.rsqrt(jnp.mean(widened * widened, axis=-1, keepdims=True) + 1e-06)
    normed = (widened * inv_rms * norm_gain).astype(jnp.bfloat16)
    projected = jnp.einsum(
        "rtd,dkc->rtkc", normed, in_projection, preferred_element_type=jnp.float32
    ).astype(jnp.bfloat16)
    rim_rows = from_behind(projected[:, -2:], "seq", 1)
    extended = jnp.concatenate([rim_rows, projected], axis=1).astype(jnp.float32)
    streams = (
        short_kernel[0] * extended[:, 2:]
        + short_kernel[1] * extended[:, 1:-1]
        + short_kernel[2] * extended[:, :-2]
    )
    query_gate = streams[:, :, 0]
    gated_source = (streams[:, :, 1] * streams[:, :, 2]).astype(jnp.bfloat16)
    record_count = gated_source.shape[0]
    block_len = gated_source.shape[1]
    channels = gated_source.shape[2]
    all_taps = lax.all_gather(long_filter, "seq", axis=1, tiled=True)
    taps_padded = jnp.concatenate(
        [jnp.zeros((all_taps.shape[0], block_len), jnp.bfloat16), all_taps], axis=1
    )
    my_start = lax.axis_index("seq") * block_len
    cycle_stops = lax.axis_size("seq")
    long_sum = block_terms(taps_padded, 0, gated_source, block_len)

    def advance(stop_index, state):
        running_sum, visiting = state
        visiting = from_behind(visiting, "seq", 1)
        lag_start = stop_index * block_len
        running_sum = lax.cond(
            lag_start <= my_start,
            lambda running: running + block_terms(taps_padded, lag_start, visiting, block_len),
            lambda running: running,
            running_sum,
        )
        return (running_sum, visiting)

    long_sum, visiting = lax.fori_loop(1, cycle_stops, advance, (long_sum, gated_source))
    long_out = long_sum.reshape(
        record_count, block_len, channels
    ) + skip_gain * gated_source.astype(jnp.float32)
    gated = (query_gate * long_out).astype(jnp.bfloat16)
    partial_terms = jnp.einsum(
        "rtc,cd->rtd", gated, out_projection, preferred_element_type=jnp.float32
    )
    return lax.psum_scatter(
        partial_terms.astype(jnp.bfloat16), "chan", scatter_dimension=2, tiled=True
    )


def solution(mesh):
    placed = (
        P("parts", "seq", "chan"),
        P(),
        P(None, None, "chan"),
        P(None, None, "chan"),
        P("chan", "seq"),
        P("chan"),
        P("chan", None),
    )
    return jax.shard_map(
        body, mesh=mesh, in_specs=placed, out_specs=P("parts", "seq", "chan"), check_vma=False
    )
```

profile of v0, /device:TPU:0, one launch (start us, length us, event | category | flops | bytes accessed | tf_op | source)
XLA Modules:
  0.0 202.3 jit_solution(438159001702864460)
XLA Ops:
  7.3 14.9 %all_gather.7 = bf16[4,1536]{1,0:T(4,128)(2,1)S(1)} all-gather(bf16[4,384]{1,0:T(4,128)(2,1)} %param.15), channel_id=1, replica_groups=mesh['parts'=2,'seq'=4,'chan'=4] {'seq'}, dimensions={1}, use_global_device_ids=true | all-gather | bytes 15360 | tf_op jit(solution)/shard_map/all_gather | solution.py:46
  23.0 8.4 %all-gather.2.cloned.1.call-done = bf16[4,384,512]{2,1,0:T(8,128)(2,1)} async-done(((bf16[4,384,128]{2,1,0:T(8,128)(2,1)}), bf16[4,384,512]{2,1,0:T(8,128)(2,1)}) %all-gather.2.cloned.1.call-update) | async-done | bytes 1572880 | tf_op jit(solution)/shard_map/all_gather | solution.py:27
  31.5 1.8 fusion.2
  33.3 2.4 %fusion.12 = bf16[4,384,3,128]{3,1,2,0:T(8,128)(2,1)S(1)} fusion(bf16[4,384,512]{2,1,0:T(8,128)(2,1)} %all-gather.2.cloned.1.call-done, f32[512]{0:T(512)S(1)} %copy-done.9, f32[4,384]{1,0:T(4,128)S(1)} %add_rsqrt_fusion, bf16[512,3,128]{2,0,1:T(8,128)(2,1)S(1)} %copy-done), kind=kOutput, calls=%fused_computation.19 | convolution fusion | flops 607715328 | bytes 3153920 | tf_op jit(solution)/shard_map/rtd,dkc->rtkc/dot_general | solution.py:31
  35.8 3.4 %collective-permute-start.1 = (bf16[4,2,3,128]{3,1,2,0:T(2,128)(2,1)S(1)}, bf16[4,2,3,128]{3,1,2,0:T(2,128)(2,1)S(1)}, u32[]{:S(2)}, u32[]{:S(2)}) collective-permute-start(bf16[4,2,3,128]{3,1,2,0:T(2,128)(2,1)S(1)} %slice.56), channel_id=1, source_target_pairs={{0,4},{4,8},{8,12},{1,5},{5,9},{9,13},{2,6},{6,10},{10,14},{3,7},{... | collective-permute-start | bytes 18440 | tf_op jit(solution)/shard_map/ppermute | solution.py:10
  39.2 1.8 copy.32
  41.1 2.8 %slice.63 = bf16[4,294528]{1,0:T(4,128)(2,1)} slice(bf16[4,294912]{1,0:T(4,128)(2,1)S(1)} %bitcast.67), slice={[0:4], [383:294911]} | slice | bytes 4712448 | tf_op jit(solution)/shard_map/slice | solution.py:19
  43.9 3.3 %reshape.52 = bf16[1178112]{0:T(1024)(128)(2,1)S(1)} reshape(bf16[4,294528]{1,0:T(4,128)(2,1)} %slice.63) | data formatting | bytes 4712448
  47.2 6.5 %reshape.40 = bf16[4,384,767]{2,1,0:T(8,128)(2,1)} reshape(bf16[1178112]{0:T(1024)(128)(2,1)S(1)} %reshape.52) | data formatting | bytes 4712448 | tf_op jit(solution)/shard_map/reshape | solution.py:20
  53.7 1.5 maximum_convert_fusion
  56.0 1.3 copy-done.1
  57.3 0.8 fusion.25
  58.4 1.9 copy.23
  60.3 1.4 convolution_bitcast_fusion
  61.7 57.2 %while.18 = (s32[]{:T(128)}, f32[4,384,4,32]{1,3,0,2:T(8,128)}, bf16[4,384,128]{1,2,0:T(8,128)(2,1)}, s32[]{:T(128)}, bf16[4,1920]{1,0:T(4,128)(2,1)S(1)}, /*index=5*/s32[]{:T(128)}, s32[]{:T(128)}) while((s32[]{:T(128)}, f32[4,384,4,32]{1,3,0,2:T(8,128)}, bf16[4,384,128]{1,2,0:T(8,128)(2,1)}, s32[]{:T(128)}, bf16[4,1920]{1,0:T(4,128)(2,1)S(1)}, ...), condition=%wide.region_4.5_spmd, body=%wide.region_1.4_spmd.sunk | while | flops 151191552 | bytes 29135044 | solution.py:66
  61.7 3.4 %collective-permute-start = (bf16[4,384,128]{1,2,0:T(8,128)(2,1)}, bf16[4,384,128]{1,2,0:T(8,128)(2,1)S(1)}, u32[]{:S(2)}, u32[]{:S(2)}) collective-permute-start(bf16[4,384,128]{1,2,0:T(8,128)(2,1)} %get-tuple-element.183), channel_id=1, source_target_pairs={{0,4},{4,8},{8,12},{1,5},{5,9},{9,13},{2,6},{6,10},{10,14},{3,7},{... | collective-permute-start | bytes 1179656 | tf_op jit(solution)/shard_map/while/body/eval_jaxpr/ppermute | solution.py:10
  65.1 8.8 %collective-permute-done = bf16[4,384,128]{1,2,0:T(8,128)(2,1)S(1)} collective-permute-done((bf16[4,384,128]{1,2,0:T(8,128)(2,1)}, bf16[4,384,128]{1,2,0:T(8,128)(2,1)S(1)}, u32[]{:S(2)}, u32[]{:S(2)}) %collective-permute-start) | collective-permute-done | bytes 393248 | tf_op jit(solution)/shard_map/while/body/eval_jaxpr/ppermute | solution.py:10
  73.9 0.8 copy.46
  74.7 23.5 %collective-permute-start = (bf16[4,384,128]{1,2,0:T(8,128)(2,1)}, bf16[4,384,128]{1,2,0:T(8,128)(2,1)S(1)}, u32[]{:S(2)}, u32[]{:S(2)}) collective-permute-start(bf16[4,384,128]{1,2,0:T(8,128)(2,1)} %get-tuple-element.183), channel_id=1, source_target_pairs={{0,4},{4,8},{8,12},{1,5},{5,9},{9,13},{2,6},{6,10},{10,14},{3,7},{... | collective-permute-start | bytes 1179656 | tf_op jit(solution)/shard_map/while/body/eval_jaxpr/ppermute | solution.py:10
  98.2 7.9 %collective-permute-done = bf16[4,384,128]{1,2,0:T(8,128)(2,1)S(1)} collective-permute-done((bf16[4,384,128]{1,2,0:T(8,128)(2,1)}, bf16[4,384,128]{1,2,0:T(8,128)(2,1)S(1)}, u32[]{:S(2)}, u32[]{:S(2)}) %collective-permute-start) | collective-permute-done | bytes 393248 | tf_op jit(solution)/shard_map/while/body/eval_jaxpr/ppermute | solution.py:10
  106.1 0.8 copy.46
  106.9 4.3 %collective-permute-start = (bf16[4,384,128]{1,2,0:T(8,128)(2,1)}, bf16[4,384,128]{1,2,0:T(8,128)(2,1)S(1)}, u32[]{:S(2)}, u32[]{:S(2)}) collective-permute-start(bf16[4,384,128]{1,2,0:T(8,128)(2,1)} %get-tuple-element.183), channel_id=1, source_target_pairs={{0,4},{4,8},{8,12},{1,5},{5,9},{9,13},{2,6},{6,10},{10,14},{3,7},{... | collective-permute-start | bytes 1179656 | tf_op jit(solution)/shard_map/while/body/eval_jaxpr/ppermute | solution.py:10
  111.2 7.0 %collective-permute-done = bf16[4,384,128]{1,2,0:T(8,128)(2,1)S(1)} collective-permute-done((bf16[4,384,128]{1,2,0:T(8,128)(2,1)}, bf16[4,384,128]{1,2,0:T(8,128)(2,1)S(1)}, u32[]{:S(2)}, u32[]{:S(2)}) %collective-permute-start) | collective-permute-done | bytes 393248 | tf_op jit(solution)/shard_map/while/body/eval_jaxpr/ppermute | solution.py:10
  118.2 0.8 copy.46
  118.9 1.2 copy.24
  120.2 1.2 copy.25
  121.4 1.9 convolution_convert_fusion
  123.3 1.4 copy.28
  124.8 1.4 copy.33
  126.2 67.1 %reduce-scatter.4.cloned.1.call-done = bf16[128,1536]{1,0:T(8,128)(2,1)} async-done(((bf16[512,1536]{1,0:T(8,128)(2,1)}), bf16[128,1536]{1,0:T(8,128)(2,1)}) %reduce-scatter.4.cloned.1.call-update) | async-done | bytes 393232
  193.4 1.1 reshape.49
  194.4 1.0 copy.29
  (39 shorter events, 2.7 us)
Async XLA Ops:
  6.5 26.8 %copy-start = (bf16[512,3,128]{2,0,1:T(8,128)(2,1)S(1)}, bf16[512,3,128]{2,0,1:T(8,128)(2,1)}, u32[]{:S(2)}) copy-start(bf16[512,3,128]{2,0,1:T(8,128)(2,1)} %param.13) | copy-start | bytes 1179652
  6.5 26.8 %copy-start.9 = (f32[512]{0:T(512)S(1)}, f32[512]{0:T(512)}, u32[]{:S(2)}) copy-start(f32[512]{0:T(512)} %param.12) | copy-start | bytes 6148
  6.5 24.9 %all-gather.2.cloned.1.call-start = ((), (), s32[]{:S(2)}) async-start(), calls=%async_computation.1 | async-start | bytes 1966080 | tf_op jit(solution)/shard_map/all_gather | solution.py:27
  7.3 186.1 %reduce-scatter.4.cloned.1.call-start = ((), (), s32[]{:S(2)}) async-start(), calls=%async_computation.2 | async-start | bytes 1966080
  33.3 5.9 %copy-start.7 = (f32[3,3,128]{2,1,0:T(4,128)S(1)}, f32[3,3,128]{2,1,0:T(4,128)}, u32[]{:S(2)}) copy-start(f32[3,3,128]{2,1,0:T(4,128)} %param.14) | copy-start | bytes 13828
  35.8 3.5 %copy-start.5 = (bf16[4,384,3,128]{3,1,2,0:T(8,128)(2,1)}, bf16[4,384,3,128]{3,1,2,0:T(8,128)(2,1)S(1)}, u32[]{:S(2)}) copy-start(bf16[4,384,3,128]{3,1,2,0:T(8,128)(2,1)S(1)} %fusion.12) | copy-start | bytes 3538948
  35.8 17.9 %collective-permute-start.1 = (bf16[4,2,3,128]{3,1,2,0:T(2,128)(2,1)S(1)}, bf16[4,2,3,128]{3,1,2,0:T(2,128)(2,1)S(1)}, u32[]{:S(2)}, u32[]{:S(2)}) collective-permute-start(bf16[4,2,3,128]{3,1,2,0:T(2,128)(2,1)S(1)} %slice.56), channel_id=1, source_target_pairs={{0,4},{4,8},{8,12},{1,5},{5,9},{9,13},{2,6},{6,10},{10,14},{3,7},{... | collective-permute-start | bytes 18440 | tf_op jit(solution)/shard_map/ppermute | solution.py:10
  55.9 1.4 copy-start.1
  55.9 4.4 %copy-start.2 = (bf16[4,384,767]{2,1,0:T(8,128)(2,1)S(1)}, bf16[4,384,767]{2,1,0:T(8,128)(2,1)}, u32[]{:S(2)}) copy-start(bf16[4,384,767]{2,1,0:T(8,128)(2,1)} %reshape.40) | copy-start | bytes 7068676
  57.3 4.4 %copy-start.3 = (bf16[4,384,1,128]{3,1,2,0:T(8,128)(2,1)}, bf16[4,384,1,128]{3,1,2,0:T(8,128)(2,1)S(1)}, u32[]{:S(2)}) copy-start(bf16[4,384,1,128]{3,1,2,0:T(8,128)(2,1)S(1)} %fusion.15) | copy-start | bytes 1179652
  61.7 12.2 %collective-permute-start = (bf16[4,384,128]{1,2,0:T(8,128)(2,1)}, bf16[4,384,128]{1,2,0:T(8,128)(2,1)S(1)}, u32[]{:S(2)}, u32[]{:S(2)}) collective-permute-start(bf16[4,384,128]{1,2,0:T(8,128)(2,1)} %get-tuple-element.183), channel_id=1, source_target_pairs={{0,4},{4,8},{8,12},{1,5},{5,9},{9,13},{2,6},{6,10},{10,14},{3,7},{... | collective-permute-start | bytes 1179656 | tf_op jit(solution)/shard_map/while/body/eval_jaxpr/ppermute | solution.py:10
  74.7 31.5 %collective-permute-start = (bf16[4,384,128]{1,2,0:T(8,128)(2,1)}, bf16[4,384,128]{1,2,0:T(8,128)(2,1)S(1)}, u32[]{:S(2)}, u32[]{:S(2)}) collective-permute-start(bf16[4,384,128]{1,2,0:T(8,128)(2,1)} %get-tuple-element.183), channel_id=1, source_target_pairs={{0,4},{4,8},{8,12},{1,5},{5,9},{9,13},{2,6},{6,10},{10,14},{3,7},{... | collective-permute-start | bytes 1179656 | tf_op jit(solution)/shard_map/while/body/eval_jaxpr/ppermute | solution.py:10
  106.9 11.3 %collective-permute-start = (bf16[4,384,128]{1,2,0:T(8,128)(2,1)}, bf16[4,384,128]{1,2,0:T(8,128)(2,1)S(1)}, u32[]{:S(2)}, u32[]{:S(2)}) collective-permute-start(bf16[4,384,128]{1,2,0:T(8,128)(2,1)} %get-tuple-element.183), channel_id=1, source_target_pairs={{0,4},{4,8},{8,12},{1,5},{5,9},{9,13},{2,6},{6,10},{10,14},{3,7},{... | collective-permute-start | bytes 1179656 | tf_op jit(solution)/shard_map/while/body/eval_jaxpr/ppermute | solution.py:10
  118.9 2.4 %copy-start.4 = (bf16[4,384,1,128]{3,1,2,0:T(8,128)(2,1)S(1)}, bf16[4,384,1,128]{3,1,2,0:T(8,128)(2,1)}, u32[]{:S(2)}) copy-start(bf16[4,384,1,128]{3,1,2,0:T(8,128)(2,1)} %copy-done.3) | copy-start | bytes 1179652
  118.9 2.4 %copy-start.6 = (bf16[128,512]{1,0:T(8,128)(2,1)S(1)}, bf16[128,512]{1,0:T(8,128)(2,1)}, u32[]{:S(2)}) copy-start(bf16[128,512]{1,0:T(8,128)(2,1)} %param.17) | copy-start | bytes 393220
  118.9 2.4 %copy-start.8 = (f32[128]{0:T(128)S(1)}, f32[128]{0:T(128)}, u32[]{:S(2)}) copy-start(f32[128]{0:T(128)} %param.16) | copy-start | bytes 1540
Sparse Core Ops, SparseCore 0:
  8.9 22.5 all-gather.1
  126.3 66.9 reduce-scatter.3
where the time goes:
time: 203 us; the launch traced here: 202 us
  waiting for transfers between devices  100 us (49%)
  starting transfers between devices  34.6 us (17%)
  local copies, waits for them, and re-layouts  28.4 us (14%)
  blocking collectives  14.9 us (7%)
  between operations  13.6 us (7%)
  matrix products  5.77 us (3%)
  other arithmetic  4.91 us (2%)
    unnamed x3, waiting for transfers between devices  67.9 us
    ppermute x4, starting transfers between devices, from_behind(): return lax.ppermute(block, axis, route)  34.6 us
    ppermute x4, waiting for transfers between devices, from_behind(): return lax.ppermute(block, axis, route)  23.7 us
    all_gather x1, blocking collectives, body(): all_taps = lax.all_gather(long_filter, 'seq', axis=1, tiled=True)  14.9 us
    unnamed x29, local copies, waits for them, and re-layouts  12.2 us
    all_gather x1, waiting for transfers between devices, body(): gathered = lax.all_gather(records, 'chan', axis=2, tiled=True)  8.44 us
    reshape x1, local copies, waits for them, and re-layouts, block_terms(): toeplitz.reshape(filter_count, block_len, 2 * block_len - 1)  6.49 us
  transfers between devices with their start and end apart: 6, of which 5 were waited for; matrix products, arithmetic and copies ran while one was open for 8% of the time, Pallas kernels for 0%

commit v1 on v0

--- a/solution.py
+++ b/solution.py
@@ -24,7 +24,12 @@
 
 
 def body(records, norm_gain, in_projection, short_kernel, long_filter, skip_gain, out_projection):
-    gathered = lax.all_gather(records, "chan", axis=2, tiled=True)
+    ring = [records]
+    for hop in range(3):
+        ring.append(lax.ppermute(ring[-1], "chan", [(dev, (dev + 1) % 4) for dev in range(4)]))
+    gathered = jnp.roll(
+        jnp.concatenate(ring[::-1], axis=2), (lax.axis_index("chan") + 1) * ring[0].shape[2], axis=2
+    )
     widened = gathered.astype(jnp.float32)
     inv_rms = lax.rsqrt(jnp.mean(widened * widened, axis=-1, keepdims=True) + 1e-06)
     normed = (widened * inv_rms * norm_gain).astype(jnp.bfloat16)

time: 203 us -> 202 us (level)
    ppermute x0 -> x3, waiting for transfers between devices: none -> 13.9 us  [body(): lax.ppermute(ring[-1], 'chan', [(dev, (dev + 1) % 4) for dev in range(4)])]
    all_gather x1 -> x0, waiting for transfers between devices: 8.44 us -> none  [body(): gathered = lax.all_gather(records, 'chan', axis=2, tiled=True)]
    ppermute x4, waiting for transfers between devices: 23.7 us -> 20.8 us  [from_behind(): return lax.ppermute(block, axis, route)]
    unnamed x29 -> x38, local copies, waits for them, and re-layouts: 12.2 us -> 13.1 us
    unnamed x3 -> x2, waiting for transfers between devices: 67.9 us -> 67.6 us
  transfers between devices with their start and end apart: 6 -> 8, of which waited for: 5 -> 6; matrix products, arithmetic and copies ran while one was open for 8% -> 8% of each run, Pallas kernels for 0% -> 0%
where the time goes in v1:
time: 202 us
  waiting for transfers between devices  102 us (50%)
  starting transfers between devices  34.1 us (17%)
  local copies, waits for them, and re-layouts  29.4 us (15%)
  blocking collectives  14.2 us (7%)
  between operations  13.7 us (7%)
  matrix products  4.38 us (2%)
  other arithmetic  3.51 us (2%)
    unnamed x2, waiting for transfers between devices  67.6 us
    ppermute x4, starting transfers between devices, from_behind(): return lax.ppermute(block, axis, route)  33.5 us
    ppermute x4, waiting for transfers between devices, from_behind(): return lax.ppermute(block, axis, route)  20.8 us
    all_gather x1, blocking collectives, body(): all_taps = lax.all_gather(long_filter, 'seq', axis=1, tiled=True)  14.2 us
    ppermute x3, waiting for transfers between devices, body(): lax.ppermute(ring[-1], 'chan', [(dev, (dev + 1) % 4) for dev in range(4)])  13.9 us
    unnamed x38, local copies, waits for them, and re-layouts  13.1 us
    reshape x1, local copies, waits for them, and re-layouts, block_terms(): toeplitz.reshape(filter_count, block_len, 2 * block_len - 1)  6.48 us
  transfers between devices with their start and end apart: 8, of which 6 were waited for; matrix products, arithmetic and copies ran while one was open for 8% of the time, Pallas kernels for 0%

profile of v1, /device:TPU:0, one launch (start us, length us, event | category | flops | bytes accessed | tf_op | source)
XLA Modules:
  0.0 201.6 jit_solution(10870840893463865665)
XLA Ops:
  7.0 7.6 %collective-permute-done.1 = bf16[4,384,128]{2,1,0:T(8,128)(2,1)S(1)} collective-permute-done((bf16[4,384,128]{2,1,0:T(8,128)(2,1)}, bf16[4,384,128]{2,1,0:T(8,128)(2,1)S(1)}, u32[]{:S(2)}, u32[]{:S(2)}) %collective-permute-start.1) | collective-permute-done | bytes 393248 | tf_op jit(solution)/shard_map/ppermute | solution.py:29
  14.6 14.2 %all_gather.3 = bf16[4,1536]{1,0:T(4,128)(2,1)S(1)} all-gather(bf16[4,384]{1,0:T(4,128)(2,1)} %param.15), channel_id=1, replica_groups=mesh['parts'=2,'seq'=4,'chan'=4] {'seq'}, dimensions={1}, use_global_device_ids=true | all-gather | bytes 15360 | tf_op jit(solution)/shard_map/all_gather | solution.py:51
  29.7 6.3 %collective-permute-done.3 = bf16[4,384,128]{2,1,0:T(8,128)(2,1)S(1)} collective-permute-done((bf16[4,384,128]{2,1,0:T(8,128)(2,1)S(1)}, bf16[4,384,128]{2,1,0:T(8,128)(2,1)S(1)}, u32[]{:S(2)}, u32[]{:S(2)}) %collective-permute-start.3) | collective-permute-done | bytes 393248 | tf_op jit(solution)/shard_map/ppermute | solution.py:29
  37.6 1.0 fusion.12
  38.7 3.7 %collective-permute-start.4 = (bf16[4,2,3,128]{3,1,2,0:T(2,128)(2,1)S(1)}, bf16[4,2,3,128]{3,1,2,0:T(2,128)(2,1)S(1)}, u32[]{:S(2)}, u32[]{:S(2)}) collective-permute-start(bf16[4,2,3,128]{3,1,2,0:T(2,128)(2,1)S(1)} %slice.56), channel_id=1, source_target_pairs={{0,4},{4,8},{8,12},{1,5},{5,9},{9,13},{2,6},{6,10},{10,14},{3,7},{... | collective-permute-start | bytes 18440 | tf_op jit(solution)/shard_map/ppermute | solution.py:10
  42.4 1.8 copy.32
  44.3 2.8 %slice.63 = bf16[4,294528]{1,0:T(4,128)(2,1)} slice(bf16[4,294912]{1,0:T(4,128)(2,1)S(1)} %bitcast.67), slice={[0:4], [383:294911]} | slice | bytes 4712448 | tf_op jit(solution)/shard_map/slice | solution.py:19
  47.0 3.3 %reshape.52 = bf16[1178112]{0:T(1024)(128)(2,1)S(1)} reshape(bf16[4,294528]{1,0:T(4,128)(2,1)} %slice.63) | data formatting | bytes 4712448
  50.3 6.5 %reshape.40 = bf16[4,384,767]{2,1,0:T(8,128)(2,1)} reshape(bf16[1178112]{0:T(1024)(128)(2,1)S(1)} %reshape.52) | data formatting | bytes 4712448 | tf_op jit(solution)/shard_map/reshape | solution.py:20
  56.8 1.5 maximum_convert_fusion
  59.1 1.3 copy-done.1
  60.5 0.8 fusion.27
  61.5 1.9 copy.23
  63.4 1.4 convolution_bitcast_fusion
  64.9 52.9 %while.18 = (s32[]{:T(128)}, f32[4,384,4,32]{1,3,0,2:T(8,128)}, bf16[4,384,128]{1,2,0:T(8,128)(2,1)}, s32[]{:T(128)}, bf16[4,1920]{1,0:T(4,128)(2,1)S(1)}, /*index=5*/s32[]{:T(128)}, s32[]{:T(128)}) while((s32[]{:T(128)}, f32[4,384,4,32]{1,3,0,2:T(8,128)}, bf16[4,384,128]{1,2,0:T(8,128)(2,1)}, s32[]{:T(128)}, bf16[4,1920]{1,0:T(4,128)(2,1)S(1)}, ...), condition=%wide.region_4.5_spmd, body=%wide.region_1.4_spmd.sunk | while | flops 151191552 | bytes 29135044 | solution.py:71
  64.9 1.9 collective-permute-start
  66.8 7.9 %collective-permute-done = bf16[4,384,128]{1,2,0:T(8,128)(2,1)S(1)} collective-permute-done((bf16[4,384,128]{1,2,0:T(8,128)(2,1)}, bf16[4,384,128]{1,2,0:T(8,128)(2,1)S(1)}, u32[]{:S(2)}, u32[]{:S(2)}) %collective-permute-start) | collective-permute-done | bytes 393248 | tf_op jit(solution)/shard_map/while/body/eval_jaxpr/ppermute | solution.py:10
  74.7 0.8 copy.53
  75.5 23.6 %collective-permute-start = (bf16[4,384,128]{1,2,0:T(8,128)(2,1)}, bf16[4,384,128]{1,2,0:T(8,128)(2,1)S(1)}, u32[]{:S(2)}, u32[]{:S(2)}) collective-permute-start(bf16[4,384,128]{1,2,0:T(8,128)(2,1)} %get-tuple-element.183), channel_id=1, source_target_pairs={{0,4},{4,8},{8,12},{1,5},{5,9},{9,13},{2,6},{6,10},{10,14},{3,7},{... | collective-permute-start | bytes 1179656 | tf_op jit(solution)/shard_map/while/body/eval_jaxpr/ppermute | solution.py:10
  99.1 6.9 %collective-permute-done = bf16[4,384,128]{1,2,0:T(8,128)(2,1)S(1)} collective-permute-done((bf16[4,384,128]{1,2,0:T(8,128)(2,1)}, bf16[4,384,128]{1,2,0:T(8,128)(2,1)S(1)}, u32[]{:S(2)}, u32[]{:S(2)}) %collective-permute-start) | collective-permute-done | bytes 393248 | tf_op jit(solution)/shard_map/while/body/eval_jaxpr/ppermute | solution.py:10
  106.0 0.8 copy.53
  106.8 4.3 %collective-permute-start = (bf16[4,384,128]{1,2,0:T(8,128)(2,1)}, bf16[4,384,128]{1,2,0:T(8,128)(2,1)S(1)}, u32[]{:S(2)}, u32[]{:S(2)}) collective-permute-start(bf16[4,384,128]{1,2,0:T(8,128)(2,1)} %get-tuple-element.183), channel_id=1, source_target_pairs={{0,4},{4,8},{8,12},{1,5},{5,9},{9,13},{2,6},{6,10},{10,14},{3,7},{... | collective-permute-start | bytes 1179656 | tf_op jit(solution)/shard_map/while/body/eval_jaxpr/ppermute | solution.py:10
  111.1 6.0 %collective-permute-done = bf16[4,384,128]{1,2,0:T(8,128)(2,1)S(1)} collective-permute-done((bf16[4,384,128]{1,2,0:T(8,128)(2,1)}, bf16[4,384,128]{1,2,0:T(8,128)(2,1)S(1)}, u32[]{:S(2)}, u32[]{:S(2)}) %collective-permute-start) | collective-permute-done | bytes 393248 | tf_op jit(solution)/shard_map/while/body/eval_jaxpr/ppermute | solution.py:10
  117.1 0.8 copy.53
  117.8 1.2 copy.24
  119.1 1.2 copy.25
  120.2 1.9 convolution_convert_fusion
  122.2 1.4 copy.28
  123.6 1.4 copy.33
  125.1 67.6 %reduce-scatter.4.cloned.1.call-done = bf16[128,1536]{1,0:T(8,128)(2,1)} async-done(((bf16[512,1536]{1,0:T(8,128)(2,1)}), bf16[128,1536]{1,0:T(8,128)(2,1)}) %reduce-scatter.4.cloned.1.call-update) | async-done | bytes 393232
  192.7 1.1 reshape.49
  193.8 1.0 copy.29
  (52 shorter events, 3.9 us)
Async XLA Ops:
  6.5 31.0 %copy-start = (bf16[512,3,128]{2,0,1:T(8,128)(2,1)S(1)}, bf16[512,3,128]{2,0,1:T(8,128)(2,1)}, u32[]{:S(2)}) copy-start(bf16[512,3,128]{2,0,1:T(8,128)(2,1)} %param.13) | copy-start | bytes 1179652
  6.5 186.2 %reduce-scatter.4.cloned.1.call-start = ((), (), s32[]{:S(2)}) async-start(), calls=%async_computation.1 | async-start | bytes 1966080
  6.5 8.0 %collective-permute-start.1 = (bf16[4,384,128]{2,1,0:T(8,128)(2,1)}, bf16[4,384,128]{2,1,0:T(8,128)(2,1)S(1)}, u32[]{:S(2)}, u32[]{:S(2)}) collective-permute-start(bf16[4,384,128]{2,1,0:T(8,128)(2,1)} %param.11), channel_id=1, source_target_pairs={{0,1},{1,2},{2,3},{3,0},{4,5},{5,6},{6,7},{7,4},{8,9},{9,10},{10,1... | collective-permute-start | bytes 1179656 | tf_op jit(solution)/shard_map/ppermute | solution.py:29
  14.6 14.2 %collective-permute-start.2 = (bf16[4,384,128]{2,1,0:T(8,128)(2,1)S(1)}, bf16[4,384,128]{2,1,0:T(8,128)(2,1)S(1)}, u32[]{:S(2)}, u32[]{:S(2)}) collective-permute-start(bf16[4,384,128]{2,1,0:T(8,128)(2,1)S(1)} %collective-permute-done.1), channel_id=1, source_target_pairs={{0,1},{1,2},{2,3},{3,0},{4,5},{5,6},{6,7},{7,4},{8,9},{9,10},{10,1... | collective-permute-start | bytes 1179656 | tf_op jit(solution)/shard_map/ppermute | solution.py:29
  28.8 7.2 %collective-permute-start.3 = (bf16[4,384,128]{2,1,0:T(8,128)(2,1)S(1)}, bf16[4,384,128]{2,1,0:T(8,128)(2,1)S(1)}, u32[]{:S(2)}, u32[]{:S(2)}) collective-permute-start(bf16[4,384,128]{2,1,0:T(8,128)(2,1)S(1)} %collective-permute-done.2), channel_id=1, source_target_pairs={{0,1},{1,2},{2,3},{3,0},{4,5},{5,6},{6,7},{7,4},{8,9},{9,10},{10,1... | collective-permute-start | bytes 1179656 | tf_op jit(solution)/shard_map/ppermute | solution.py:29
  29.6 6.9 %copy-start.5 = (bf16[4,384,128]{2,1,0:T(8,128)(2,1)S(1)}, bf16[4,384,128]{2,1,0:T(8,128)(2,1)}, u32[]{:S(2)}) copy-start(bf16[4,384,128]{2,1,0:T(8,128)(2,1)} %param.11) | copy-start | bytes 1179652
  36.6 1.0 copy-start.10
  37.6 4.8 %copy-start.8 = (f32[3,3,128]{2,1,0:T(4,128)S(1)}, f32[3,3,128]{2,1,0:T(4,128)}, u32[]{:S(2)}) copy-start(f32[3,3,128]{2,1,0:T(4,128)} %param.14) | copy-start | bytes 13828
  38.6 3.8 %copy-start.6 = (bf16[4,384,3,128]{3,1,2,0:T(8,128)(2,1)}, bf16[4,384,3,128]{3,1,2,0:T(8,128)(2,1)S(1)}, u32[]{:S(2)}) copy-start(bf16[4,384,3,128]{3,1,2,0:T(8,128)(2,1)S(1)} %fusion.12) | copy-start | bytes 3538948
  38.7 18.1 %collective-permute-start.4 = (bf16[4,2,3,128]{3,1,2,0:T(2,128)(2,1)S(1)}, bf16[4,2,3,128]{3,1,2,0:T(2,128)(2,1)S(1)}, u32[]{:S(2)}, u32[]{:S(2)}) collective-permute-start(bf16[4,2,3,128]{3,1,2,0:T(2,128)(2,1)S(1)} %slice.56), channel_id=1, source_target_pairs={{0,4},{4,8},{8,12},{1,5},{5,9},{9,13},{2,6},{6,10},{10,14},{3,7},{... | collective-permute-start | bytes 18440 | tf_op jit(solution)/shard_map/ppermute | solution.py:10
  59.0 1.4 copy-start.1
  59.0 4.4 %copy-start.2 = (bf16[4,384,767]{2,1,0:T(8,128)(2,1)S(1)}, bf16[4,384,767]{2,1,0:T(8,128)(2,1)}, u32[]{:S(2)}) copy-start(bf16[4,384,767]{2,1,0:T(8,128)(2,1)} %reshape.40) | copy-start | bytes 7068676
  60.5 4.4 %copy-start.3 = (bf16[4,384,1,128]{3,1,2,0:T(8,128)(2,1)}, bf16[4,384,1,128]{3,1,2,0:T(8,128)(2,1)S(1)}, u32[]{:S(2)}) copy-start(bf16[4,384,1,128]{3,1,2,0:T(8,128)(2,1)S(1)} %fusion.16) | copy-start | bytes 1179652
  64.9 9.9 %collective-permute-start = (bf16[4,384,128]{1,2,0:T(8,128)(2,1)}, bf16[4,384,128]{1,2,0:T(8,128)(2,1)S(1)}, u32[]{:S(2)}, u32[]{:S(2)}) collective-permute-start(bf16[4,384,128]{1,2,0:T(8,128)(2,1)} %get-tuple-element.183), channel_id=1, source_target_pairs={{0,4},{4,8},{8,12},{1,5},{5,9},{9,13},{2,6},{6,10},{10,14},{3,7},{... | collective-permute-start | bytes 1179656 | tf_op jit(solution)/shard_map/while/body/eval_jaxpr/ppermute | solution.py:10
  75.5 30.5 %collective-permute-start = (bf16[4,384,128]{1,2,0:T(8,128)(2,1)}, bf16[4,384,128]{1,2,0:T(8,128)(2,1)S(1)}, u32[]{:S(2)}, u32[]{:S(2)}) collective-permute-start(bf16[4,384,128]{1,2,0:T(8,128)(2,1)} %get-tuple-element.183), channel_id=1, source_target_pairs={{0,4},{4,8},{8,12},{1,5},{5,9},{9,13},{2,6},{6,10},{10,14},{3,7},{... | collective-permute-start | bytes 1179656 | tf_op jit(solution)/shard_map/while/body/eval_jaxpr/ppermute | solution.py:10
  106.8 10.3 %collective-permute-start = (bf16[4,384,128]{1,2,0:T(8,128)(2,1)}, bf16[4,384,128]{1,2,0:T(8,128)(2,1)S(1)}, u32[]{:S(2)}, u32[]{:S(2)}) collective-permute-start(bf16[4,384,128]{1,2,0:T(8,128)(2,1)} %get-tuple-element.183), channel_id=1, source_target_pairs={{0,4},{4,8},{8,12},{1,5},{5,9},{9,13},{2,6},{6,10},{10,14},{3,7},{... | collective-permute-start | bytes 1179656 | tf_op jit(solution)/shard_map/while/body/eval_jaxpr/ppermute | solution.py:10
  117.8 2.4 %copy-start.4 = (bf16[4,384,1,128]{3,1,2,0:T(8,128)(2,1)S(1)}, bf16[4,384,1,128]{3,1,2,0:T(8,128)(2,1)}, u32[]{:S(2)}) copy-start(bf16[4,384,1,128]{3,1,2,0:T(8,128)(2,1)} %copy-done.3) | copy-start | bytes 1179652
  117.8 2.4 %copy-start.7 = (bf16[128,512]{1,0:T(8,128)(2,1)S(1)}, bf16[128,512]{1,0:T(8,128)(2,1)}, u32[]{:S(2)}) copy-start(bf16[128,512]{1,0:T(8,128)(2,1)} %param.17) | copy-start | bytes 393220
  117.8 2.4 %copy-start.9 = (f32[128]{0:T(128)S(1)}, f32[128]{0:T(128)}, u32[]{:S(2)}) copy-start(f32[128]{0:T(128)} %param.16) | copy-start | bytes 1540
Sparse Core Ops, SparseCore 0:
  125.2 67.4 reduce-scatter.3
